TPU v7x, 512 devices: a whole 4x4x16 slice. The times are simulated.
512 devices in a mesh: dp: 32 (over y, z_lo, core), expert: 16 (over x, z_hi).
Axes of the slice: x: 4, y: 4, z: 16 (z_hi: 4, z_lo: 4; z = z_hi * 4 + z_lo), core: 2. Of those that a mesh axis runs over, the one named last changes fastest.
Arguments:
- tokens: bfloat16 [65536, 2560], P(('dp', 'expert')), may hold values from -6 to 6
- cotangent: bfloat16 [65536, 2560], P(('dp', 'expert')), may hold values from -6 to 6
- routes: int32 [65536, 6], P(('dp', 'expert')), may hold values from 0 to 159, all different within a row
- gates: float32 [65536, 6], P(('dp', 'expert')), may hold values from 0.05 to 0.5
- layout: int32 [3, 16], replicated, may hold values from 0 to 15, as said below
- weights: bfloat16 [16, 2560, 768], P('expert', 'dp'), may hold values from -0.125 to 0.125
- first_moment: float32 [16, 2560, 768], P('expert', 'dp'), may hold values from -12 to 12
- second_moment: float32 [16, 2560, 768], P('expert', 'dp'), may hold values from 0.5 to 50
Outputs:
- grad_input: bfloat16 [65536, 2560], P(('dp', 'expert'))
- new_first: float32 [16, 2560, 768], P('expert', 'dp')
- new_second: float32 [16, 2560, 768], P('expert', 'dp')
Inputs may be any that keep to these rules, and one draw needn't show every extreme that they name: `routes`: each token names 6 different experts. Row 0 is a permutation of the slots; row 1 is i XOR m for one m of 1 to 15, the same for every i, so that i and layout[1, i] form a pair; row 2 holds 0 or 1, equal for both members of a pair; some pair swaps and, where there are two pairs or more, some pair keeps its slots.
All inputs are finite; a program needn't handle non-finite values.
Results may differ from a plain program's by a relative error of at most 0.015.
Values may be sent and summed in bfloat16 or wider, within the bound.
A program may use at most 64 MiB of HBM per device.

v0:
```python
import jax
import jax.numpy as jnp
from jax import lax
from jax.sharding import Mesh
from jax.sharding import PartitionSpec as P

HSPLIT = 4
CAP = 8
DP = ("dp_0", "dp_1", "dp_2")
DP_EXPERT = ("dp_0", "dp_1", "dp_2", "expert")


first_decay = 0.9
second_decay = 0.999


def swapped(block, axis, bit):
    count = lax.axis_size(axis)
    route = []
    for low in range(count):
        high = low | 1 << bit
        if high != low and high < count:
            route += [(low, high), (high, low)]
    return lax.ppermute(block, axis, route)


def sent_together(arrays, axis, split_dim, concat_dim, along):
    ends, at = ([], 0)
    for a in arrays[:-1]:
        at += a.shape[along]
        ends.append(at)
    both = jnp.concatenate(arrays, axis=along)
    return tuple(
        jnp.split(
            lax.all_to_all(both, axis, split_axis=split_dim, concat_axis=concat_dim, tiled=True),
            ends,
            axis=along,
        )
    )


def laid_out(tiles, dim):
    lengths = list(tiles.shape[1:])
    lengths[dim] *= tiles.shape[0]
    return jnp.moveaxis(tiles, 0, dim).reshape(lengths)


def stacked_from(array, axes, sequence):
    tiles = array
    for k in sequence:
        tiles = lax.all_gather(tiles, axes[k])
    done = sequence[::-1]
    back = [done.index(k) for k in range(len(axes))]
    tiles = tiles.transpose(*back, *range(len(axes), tiles.ndim))
    return tiles.reshape(-1, *array.shape)


def whole_of(array, axes, sequence, dim):
    return laid_out(stacked_from(array, axes, sequence), dim)


def select_lane(values, lane_ids, index_now):
    return jnp.sum(jnp.where(lane_ids == index_now, values, 0))


def local(tokens, cotangent, routes, gates, layout, weights, first_moment, second_moment):
    n_expert = lax.axis_size("expert")
    own_index = lax.axis_index("expert")
    lane_ids = jnp.arange(n_expert, dtype=jnp.int32)
    placement = layout[0]
    xor_mask = layout[1, 0]
    swap_on = layout[2]
    held_slot = jnp.where(swap_on == 1, jnp.bitwise_xor(lane_ids, xor_mask), lane_ids)
    inverse = jnp.sum(
        jnp.where(placement[None, :] == lane_ids[:, None], lane_ids[None, :], 0), axis=1
    )
    slot_owner = inverse // HSPLIT
    expert_at = jnp.sum(
        jnp.where(held_slot[:, None] == lane_ids[None, :], slot_owner[None, :], 0), axis=1
    )
    active = select_lane(swap_on, lane_ids, own_index) == 1
    bit_count = n_expert.bit_length() - 1
    moved_weights = weights
    for bit_pos in range(bit_count):
        partner_copy = swapped(moved_weights, "expert", bit_pos)
        flip_now = jnp.bitwise_and(jnp.right_shift(xor_mask, bit_pos), 1) == 1
        moved_weights = jnp.where(flip_now, partner_copy, moved_weights)
    held_weights = jnp.where(active, moved_weights, weights)[0]
    moments = jnp.stack((first_moment, second_moment))
    moved_moments = moments
    for bit_pos in range(bit_count):
        partner_moments = swapped(moved_moments.astype(jnp.bfloat16), "expert", bit_pos).astype(
            moved_moments.dtype
        )
        flip_now = jnp.bitwise_and(jnp.right_shift(xor_mask, bit_pos), 1) == 1
        moved_moments = jnp.where(flip_now, partner_moments, moved_moments)
    held_moments = jnp.where(active, moved_moments, moments)[:, 0]
    n_window = n_expert // HSPLIT
    tok_dev, top_count = routes.shape
    width = tokens.shape[1]
    flat_ids = routes.reshape(-1)
    window_ids = jnp.arange(n_window, dtype=jnp.int32)
    hit_table = (flat_ids[:, None] == window_ids[None, :]).astype(jnp.int32)
    earlier = jnp.cumsum(hit_table, axis=0) - hit_table
    position = jnp.sum(earlier * hit_table, axis=1)
    kept = (flat_ids < n_window) & (position < CAP)
    slot_key = jnp.where(kept, flat_ids * CAP + position, -1)
    slot_pick = (jnp.arange(n_window * CAP, dtype=jnp.int32)[:, None] == slot_key[None, :]).astype(
        jnp.float32
    )
    assign_rows = jnp.arange(tok_dev * top_count, dtype=jnp.int32)[:, None] // top_count
    assign_token = (assign_rows == jnp.arange(tok_dev, dtype=jnp.int32)[None, :]).astype(
        jnp.float32
    )
    slot_token = jnp.dot(slot_pick, assign_token, precision=lax.Precision.HIGHEST)
    slot_gate = jnp.dot(slot_pick, gates.reshape(-1), precision=lax.Precision.HIGHEST)
    choose = (expert_at[:, None] == window_ids[None, :]).astype(jnp.float32)
    dest_token = jnp.dot(
        choose, slot_token.reshape(n_window, CAP * tok_dev), precision=lax.Precision.HIGHEST
    )
    dest_token = dest_token.reshape(n_expert * CAP, tok_dev).astype(jnp.bfloat16)
    dest_gate = jnp.dot(
        choose, slot_gate.reshape(n_window, CAP), precision=lax.Precision.HIGHEST
    ).reshape(-1, 1)
    send_rows = jnp.dot(dest_token, tokens, preferred_element_type=jnp.float32).astype(jnp.bfloat16)
    send_grads = (
        jnp.dot(dest_token, cotangent, preferred_element_type=jnp.float32) * dest_gate
    ).astype(jnp.bfloat16)
    send_rows = send_rows.reshape(n_expert, CAP, width)
    send_grads = send_grads.reshape(n_expert, CAP, width)
    recv_rows, recv_grads = sent_together((send_rows, send_grads), "expert", 0, 0, 1)
    rows_in = recv_rows.reshape(-1, width)
    grads_in = recv_grads.reshape(-1, width)
    width_dev = held_weights.shape[1] // 3
    full_weights = whole_of(held_weights, DP, (1, 0, 2), 0)
    pre_act = jnp.dot(rows_in, full_weights[:, : 2 * width_dev], preferred_element_type=jnp.float32)
    hidden_grad = jnp.dot(
        grads_in, full_weights[:, 2 * width_dev :], preferred_element_type=jnp.float32
    )
    gate_pre = pre_act[:, :width_dev]
    up_pre = pre_act[:, width_dev:]
    sigma = jax.nn.sigmoid(gate_pre)
    active_part = gate_pre * sigma
    hidden = (active_part * up_pre).astype(jnp.bfloat16)
    gate_grad = (hidden_grad * up_pre * sigma * (1.0 + gate_pre * (1.0 - sigma))).astype(
        jnp.bfloat16
    )
    up_grad = (hidden_grad * active_part).astype(jnp.bfloat16)
    both_grads = jnp.concatenate((gate_grad, up_grad), axis=1)
    part_rows = lax.dot_general(
        both_grads,
        full_weights[:, : 2 * width_dev],
        (((1,), (1,)), ((), ())),
        preferred_element_type=jnp.float32,
    )
    part_rows = part_rows.astype(jnp.bfloat16).reshape(n_expert, CAP, width)
    returned = lax.all_to_all(part_rows, "expert", split_axis=0, concat_axis=0, tiled=True)
    grad_input = lax.dot_general(
        dest_token,
        returned.reshape(-1, width),
        (((0,), (0,)), ((), ())),
        preferred_element_type=jnp.float32,
    ).astype(jnp.bfloat16)
    proj_grad = lax.dot_general(
        rows_in, both_grads, (((0,), (0,)), ((), ())), preferred_element_type=jnp.float32
    )
    down_grad = lax.dot_general(
        grads_in, hidden, (((0,), (0,)), ((), ())), preferred_element_type=jnp.float32
    )
    weight_grad = lax.psum_scatter(
        jnp.concatenate((proj_grad, down_grad), axis=1).astype(jnp.bfloat16),
        DP,
        scatter_dimension=0,
        tiled=True,
    ).astype(jnp.float32)
    new_first = first_decay * held_moments[0] + (1.0 - first_decay) * weight_grad
    new_second = second_decay * held_moments[1] + (1.0 - second_decay) * weight_grad * weight_grad
    return (grad_input, new_first[None], new_second[None])


def solution(mesh):
    split = Mesh(
        mesh.devices.reshape(4, 4, 2, mesh.shape["expert"]), ("dp_0", "dp_1", "dp_2", "expert")
    )
    in_specs = (
        P(DP_EXPERT, None),
        P(DP_EXPERT, None),
        P(DP_EXPERT, None),
        P(DP_EXPERT, None),
        P(),
        P("expert", DP, None),
        P("expert", DP, None),
        P("expert", DP, None),
    )
    out_specs = (P(DP_EXPERT, None), P("expert", DP, None), P("expert", DP, None))
    return jax.shard_map(local, mesh=split, in_specs=in_specs, out_specs=out_specs, check_vma=False)
```

profile of v0, /device:TPU:4, one launch (start us, length us, event | category | flops | bytes accessed | tf_op | source)
XLA Modules:
  0.0 386.5 jit_solution(2302566709495059458)
XLA Ops:
  7.2 9.2 %collective-permute-start = (bf16[1,80,768]{2,1,0:T(8,128)(2,1)}, bf16[1,80,768]{2,1,0:T(8,128)(2,1)S(1)}, u32[]{:S(2)}, u32[]{:S(2)}) collective-permute-start(bf16[1,80,768]{2,1,0:T(8,128)(2,1)} %param.13), channel_id=1, source_target_pairs={{0,1},{1,0},{2,3},{3,2},{4,5},{5,4},{6,7},{7,6},{8,9},{9,8},{10,11... | collective-permute-start | bytes 368648 | tf_op jit(solution)/shard_map/ppermute | solution.py:24
  16.5 0.8 copy.42
  17.4 1.1 reduce-window.6
  18.6 0.2 slice_reduce_fusion
  19.0 1.2 slice.37
  21.5 6.4 %collective-permute-done = bf16[1,80,768]{2,1,0:T(8,128)(2,1)S(1)} collective-permute-done((bf16[1,80,768]{2,1,0:T(8,128)(2,1)}, bf16[1,80,768]{2,1,0:T(8,128)(2,1)S(1)}, u32[]{:S(2)}, u32[]{:S(2)}) %collective-permute-start) | collective-permute-done | bytes 122912 | tf_op jit(solution)/shard_map/ppermute | solution.py:24
  27.9 14.2 %collective-permute-start.1 = (bf16[1,80,768]{2,1,0:T(8,128)(2,1)S(1)}, bf16[1,80,768]{2,1,0:T(8,128)(2,1)S(1)}, u32[]{:S(2)}, u32[]{:S(2)}) collective-permute-start(bf16[1,80,768]{2,1,0:T(8,128)(2,1)S(1)} %broadcast_select_fusion), channel_id=1, source_target_pairs={{0,2},{2,0},{1,3},{3,1},{4,6},{6,4},{5,7},{7,5},{8,10},{10,8},{9,1... | collective-permute-start | bytes 368648 | tf_op jit(solution)/shard_map/ppermute | solution.py:24
  42.2 4.5 %collective-permute-done.1 = bf16[1,80,768]{2,1,0:T(8,128)(2,1)S(1)} collective-permute-done((bf16[1,80,768]{2,1,0:T(8,128)(2,1)S(1)}, bf16[1,80,768]{2,1,0:T(8,128)(2,1)S(1)}, u32[]{:S(2)}, u32[]{:S(2)}) %collective-permute-start.1) | collective-permute-done | bytes 122912 | tf_op jit(solution)/shard_map/ppermute | solution.py:24
  46.7 3.1 collective-permute-start.2
  49.8 0.7 slice_bitcast_fusion.6
  51.3 2.2 collective-permute-done.2
  53.5 2.4 collective-permute-start.3
  55.9 2.0 fusion.38
  59.4 2.4 collective-permute-done.3
  61.8 16.4 %all_gather.15 = bf16[4,80,768]{2,1,0:T(8,128)(2,1)} all-gather(bf16[1,80,768]{2,1,0:T(8,128)(2,1)S(1)} %select_select_fusion.1), channel_id=1, replica_groups=mesh['dp_0'=4,'dp_1'=4,'dp_2'=2,'expert'=16] {'dp_1'}, dimensions={0}, use_global_device_ids=true | all-gather | bytes 614400 | tf_op jit(solution)/shard_map/all_gather | solution.py:51
  78.3 0.3 fusion.18
  78.8 0.2 convolution_convert_fusion.5
  79.3 0.5 fusion.22
  80.1 0.3 fusion.2
  80.5 0.3 fusion.1
  80.8 1.3 pad_maximum_fusion.1
  82.1 15.4 %all-to-all-start = ((bf16[16,16,2560]{2,1,0:T(8,128)(2,1)}), bf16[16,16,2560]{2,1,0:T(8,128)(2,1)S(1)}, u32[]{:S(2)}, u32[]{:S(2)}) async-start(bf16[16,16,2560]{2,1,0:T(8,128)(2,1)} %pad_maximum_fusion.1), calls=%async_computation | async-start | bytes 2621440 | tf_op jit(solution)/shard_map/all_to_all | solution.py:35
  97.5 22.0 %all-gather.5.cloned.1.call-done = bf16[16,80,768]{2,1,0:T(8,128)(2,1)} async-done(((bf16[4,80,768]{2,1,0:T(8,128)(2,1)}), bf16[16,80,768]{2,1,0:T(8,128)(2,1)}) %all-gather.5.cloned.1.call-update) | async-done | bytes 1966096 | tf_op jit(solution)/shard_map/all_gather | solution.py:51
  119.6 25.8 %all-gather.7.cloned.1.call-done = bf16[8,4,80,768]{3,2,1,0:T(8,128)(2,1)} async-done(((bf16[4,4,80,768]{3,2,1,0:T(8,128)(2,1)}), bf16[8,4,80,768]{3,2,1,0:T(8,128)(2,1)}) %all-gather.7.cloned.1.call-update) | async-done | bytes 3932176 | tf_op jit(solution)/shard_map/all_gather | solution.py:51
  145.4 4.4 %copy.46 = bf16[4,4,2,80,768]{4,3,2,1,0:T(8,128)(2,1)} copy(bf16[4,4,2,80,768]{4,3,1,0,2:T(8,128)(2,1)} %bitcast.87) | data formatting | bytes 7864320 | tf_op jit(solution)/shard_map/transpose | solution.py:54
  149.8 2.3 fusion.5
  152.1 1.7 multiply_convert_fusion.2
  153.8 0.6 convolution_convert_fusion.1
  154.3 0.9 convolution_convert_fusion
  155.2 2.2 pad_maximum_fusion
  157.4 6.3 %copy.53 = bf16[2560,768]{1,0:T(8,128)(2,1)} copy(bf16[2560,768]{0,1:T(8,128)(2,1)} %pad_maximum_fusion) | data formatting | bytes 7864320
  163.8 3.6 fusion.3
  167.4 15.2 %all-to-all-start.1 = ((bf16[16,8,2560]{2,1,0:T(8,128)(2,1)}), bf16[16,8,2560]{2,1,0:T(8,128)(2,1)S(1)}, u32[]{:S(2)}, u32[]{:S(2)}) async-start(bf16[16,8,2560]{2,1,0:T(8,128)(2,1)} %fusion.3), calls=%async_computation.1 | async-start | bytes 1310720 | tf_op jit(solution)/shard_map/all_to_all | solution.py:157
  182.9 7.3 %collective-permute-start.4 = (bf16[2,1,80,768]{2,3,1,0:T(8,128)(2,1)S(1)}, bf16[2,1,80,768]{2,3,1,0:T(8,128)(2,1)S(1)}, u32[]{:S(2)}, u32[]{:S(2)}) collective-permute-start(bf16[2,1,80,768]{2,3,1,0:T(8,128)(2,1)S(1)} %fusion.19), channel_id=1, source_target_pairs={{0,1},{1,0},{2,3},{3,2},{4,5},{5,4},{6,7},{7,6},{8,9},{9,8},{10,11... | collective-permute-start | bytes 737288 | tf_op jit(solution)/shard_map/ppermute | solution.py:24
  190.2 51.9 %collective-permute-done.4 = bf16[2,1,80,768]{2,3,1,0:T(8,128)(2,1)S(1)} collective-permute-done((bf16[2,1,80,768]{2,3,1,0:T(8,128)(2,1)S(1)}, bf16[2,1,80,768]{2,3,1,0:T(8,128)(2,1)S(1)}, u32[]{:S(2)}, u32[]{:S(2)}) %collective-permute-start.4) | collective-permute-done | bytes 245792 | tf_op jit(solution)/shard_map/ppermute | solution.py:24
  242.3 6.1 %collective-permute-start.5 = (bf16[2,1,80,768]{2,3,1,0:T(8,128)(2,1)S(1)}, bf16[2,1,80,768]{2,3,1,0:T(8,128)(2,1)S(1)}, u32[]{:S(2)}, u32[]{:S(2)}) collective-permute-start(bf16[2,1,80,768]{2,3,1,0:T(8,128)(2,1)S(1)} %fusion.10), channel_id=1, source_target_pairs={{0,2},{2,0},{1,3},{3,1},{4,6},{6,4},{5,7},{7,5},{8,10},{10,8},{9,1... | collective-permute-start | bytes 737288 | tf_op jit(solution)/shard_map/ppermute | solution.py:24
  248.4 17.1 %collective-permute-done.5 = bf16[2,1,80,768]{2,3,1,0:T(8,128)(2,1)S(1)} collective-permute-done((bf16[2,1,80,768]{2,3,1,0:T(8,128)(2,1)S(1)}, bf16[2,1,80,768]{2,3,1,0:T(8,128)(2,1)S(1)}, u32[]{:S(2)}, u32[]{:S(2)}) %collective-permute-start.5) | collective-permute-done | bytes 245792 | tf_op jit(solution)/shard_map/ppermute | solution.py:24
  265.6 3.0 collective-permute-start.6
  268.6 8.4 %collective-permute-done.6 = bf16[2,1,80,768]{2,3,1,0:T(8,128)(2,1)S(1)} collective-permute-done((bf16[2,1,80,768]{2,3,1,0:T(8,128)(2,1)S(1)}, bf16[2,1,80,768]{2,3,1,0:T(8,128)(2,1)S(1)}, u32[]{:S(2)}, u32[]{:S(2)}) %collective-permute-start.6) | collective-permute-done | bytes 245792 | tf_op jit(solution)/shard_map/ppermute | solution.py:24
  277.0 0.2 fusion.11
  277.2 4.7 %collective-permute-start.7 = (bf16[2,1,80,768]{2,3,1,0:T(8,128)(2,1)S(1)}, bf16[2,1,80,768]{2,3,1,0:T(8,128)(2,1)S(1)}, u32[]{:S(2)}, u32[]{:S(2)}) collective-permute-start(bf16[2,1,80,768]{2,3,1,0:T(8,128)(2,1)S(1)} %fusion.11), channel_id=1, source_target_pairs={{0,8},{8,0},{1,9},{9,1},{2,10},{10,2},{3,11},{11,3},{4,12},{12,4},... | collective-permute-start | bytes 737288 | tf_op jit(solution)/shard_map/ppermute | solution.py:24
  282.0 7.4 %collective-permute-done.7 = bf16[2,1,80,768]{2,3,1,0:T(8,128)(2,1)S(1)} collective-permute-done((bf16[2,1,80,768]{2,3,1,0:T(8,128)(2,1)S(1)}, bf16[2,1,80,768]{2,3,1,0:T(8,128)(2,1)S(1)}, u32[]{:S(2)}, u32[]{:S(2)}) %collective-permute-start.7) | collective-permute-done | bytes 245792 | tf_op jit(solution)/shard_map/ppermute | solution.py:24
  289.4 0.3 select_select_fusion
  289.7 1.2 convolution_convert_fusion.2
  290.9 86.2 %reduce-scatter.4.cloned.1.call-done = bf16[80,768]{1,0:T(8,128)(2,1)} async-done(((bf16[2560,768]{1,0:T(8,128)(2,1)}), bf16[80,768]{1,0:T(8,128)(2,1)}) %reduce-scatter.4.cloned.1.call-update) | async-done | bytes 122896
  377.1 1.1 copy.54
  378.2 0.8 copy.49
  379.1 0.8 copy.50
  (44 shorter events, 2.5 us)
Async XLA Ops:
  7.2 73.0 %copy-start = (bf16[128,2560]{1,0:T(8,128)(2,1)S(1)}, bf16[128,2560]{1,0:T(8,128)(2,1)}, u32[]{:S(2)}) copy-start(bf16[128,2560]{1,0:T(8,128)(2,1)} %param.8) | copy-start | bytes 1966084
  7.2 71.9 %copy-start.4 = (f32[128,6]{0,1:T(8,128)S(1)}, f32[128,6]{0,1:T(8,128)}, u32[]{:S(2)}) copy-start(f32[128,6]{0,1:T(8,128)} %param.11) | copy-start | bytes 9220
  7.2 73.3 %copy-start.1 = (bf16[128,2560]{1,0:T(8,128)(2,1)S(1)}, bf16[128,2560]{1,0:T(8,128)(2,1)}, u32[]{:S(2)}) copy-start(bf16[128,2560]{1,0:T(8,128)(2,1)} %param.9) | copy-start | bytes 1966084
  7.2 112.3 %all-gather.5.cloned.1.call-start = ((), (), s32[]{:S(2)}) async-start(), calls=%async_computation.3 | async-start | bytes 2457600 | tf_op jit(solution)/shard_map/all_gather | solution.py:51
  7.2 20.7 %collective-permute-start = (bf16[1,80,768]{2,1,0:T(8,128)(2,1)}, bf16[1,80,768]{2,1,0:T(8,128)(2,1)S(1)}, u32[]{:S(2)}, u32[]{:S(2)}) collective-permute-start(bf16[1,80,768]{2,1,0:T(8,128)(2,1)} %param.13), channel_id=1, source_target_pairs={{0,1},{1,0},{2,3},{3,2},{4,5},{5,4},{6,7},{7,6},{8,9},{9,8},{10,11... | collective-permute-start | bytes 368648 | tf_op jit(solution)/shard_map/ppermute | solution.py:24
  27.9 18.8 %collective-permute-start.1 = (bf16[1,80,768]{2,1,0:T(8,128)(2,1)S(1)}, bf16[1,80,768]{2,1,0:T(8,128)(2,1)S(1)}, u32[]{:S(2)}, u32[]{:S(2)}) collective-permute-start(bf16[1,80,768]{2,1,0:T(8,128)(2,1)S(1)} %broadcast_select_fusion), channel_id=1, source_target_pairs={{0,2},{2,0},{1,3},{3,1},{4,6},{6,4},{5,7},{7,5},{8,10},{10,8},{9,1... | collective-permute-start | bytes 368648 | tf_op jit(solution)/shard_map/ppermute | solution.py:24
  46.7 6.8 %collective-permute-start.2 = (bf16[1,80,768]{2,1,0:T(8,128)(2,1)S(1)}, bf16[1,80,768]{2,1,0:T(8,128)(2,1)S(1)}, u32[]{:S(2)}, u32[]{:S(2)}) collective-permute-start(bf16[1,80,768]{2,1,0:T(8,128)(2,1)S(1)} %broadcast_select_fusion.1), channel_id=1, source_target_pairs={{0,4},{4,0},{1,5},{5,1},{2,6},{6,2},{3,7},{7,3},{8,12},{12,8},{9,1... | collective-permute-start | bytes 368648 | tf_op jit(solution)/shard_map/ppermute | solution.py:24
  53.5 8.3 %collective-permute-start.3 = (bf16[1,80,768]{2,1,0:T(8,128)(2,1)S(1)}, bf16[1,80,768]{2,1,0:T(8,128)(2,1)S(1)}, u32[]{:S(2)}, u32[]{:S(2)}) collective-permute-start(bf16[1,80,768]{2,1,0:T(8,128)(2,1)S(1)} %broadcast_select_fusion.2), channel_id=1, source_target_pairs={{0,8},{8,0},{1,9},{9,1},{2,10},{10,2},{3,11},{11,3},{4,12},{12,4},... | collective-permute-start | bytes 368648 | tf_op jit(solution)/shard_map/ppermute | solution.py:24
  82.1 67.8 %all-to-all-start = ((bf16[16,16,2560]{2,1,0:T(8,128)(2,1)}), bf16[16,16,2560]{2,1,0:T(8,128)(2,1)S(1)}, u32[]{:S(2)}, u32[]{:S(2)}) async-start(bf16[16,16,2560]{2,1,0:T(8,128)(2,1)} %pad_maximum_fusion.1), calls=%async_computation | async-start | bytes 2621440 | tf_op jit(solution)/shard_map/all_to_all | solution.py:35
  97.5 47.9 %all-gather.7.cloned.1.call-start = ((), (), s32[]{:S(2)}) async-start(), calls=%async_computation.4 | async-start | bytes 5898240 | tf_op jit(solution)/shard_map/all_gather | solution.py:51
  119.5 257.5 %reduce-scatter.4.cloned.1.call-start = ((), (), s32[]{:S(2)}) async-start(), calls=%async_computation.5 | async-start | bytes 4055040
  163.7 18.8 %copy-start.2 = (f32[1,80,768]{2,1,0:T(8,128)S(1)}, f32[1,80,768]{2,1,0:T(8,128)}, u32[]{:S(2)}) copy-start(f32[1,80,768]{2,1,0:T(8,128)} %param.15) | copy-start | bytes 737284
  163.7 19.0 %copy-start.3 = (f32[1,80,768]{2,1,0:T(8,128)S(1)}, f32[1,80,768]{2,1,0:T(8,128)}, u32[]{:S(2)}) copy-start(f32[1,80,768]{2,1,0:T(8,128)} %param.14) | copy-start | bytes 737284
  167.4 122.3 %all-to-all-start.1 = ((bf16[16,8,2560]{2,1,0:T(8,128)(2,1)}), bf16[16,8,2560]{2,1,0:T(8,128)(2,1)S(1)}, u32[]{:S(2)}, u32[]{:S(2)}) async-start(bf16[16,8,2560]{2,1,0:T(8,128)(2,1)} %fusion.3), calls=%async_computation.1 | async-start | bytes 1310720 | tf_op jit(solution)/shard_map/all_to_all | solution.py:157
  182.9 59.2 %collective-permute-start.4 = (bf16[2,1,80,768]{2,3,1,0:T(8,128)(2,1)S(1)}, bf16[2,1,80,768]{2,3,1,0:T(8,128)(2,1)S(1)}, u32[]{:S(2)}, u32[]{:S(2)}) collective-permute-start(bf16[2,1,80,768]{2,3,1,0:T(8,128)(2,1)S(1)} %fusion.19), channel_id=1, source_target_pairs={{0,1},{1,0},{2,3},{3,2},{4,5},{5,4},{6,7},{7,6},{8,9},{9,8},{10,11... | collective-permute-start | bytes 737288 | tf_op jit(solution)/shard_map/ppermute | solution.py:24
  242.3 23.2 %collective-permute-start.5 = (bf16[2,1,80,768]{2,3,1,0:T(8,128)(2,1)S(1)}, bf16[2,1,80,768]{2,3,1,0:T(8,128)(2,1)S(1)}, u32[]{:S(2)}, u32[]{:S(2)}) collective-permute-start(bf16[2,1,80,768]{2,3,1,0:T(8,128)(2,1)S(1)} %fusion.10), channel_id=1, source_target_pairs={{0,2},{2,0},{1,3},{3,1},{4,6},{6,4},{5,7},{7,5},{8,10},{10,8},{9,1... | collective-permute-start | bytes 737288 | tf_op jit(solution)/shard_map/ppermute | solution.py:24
  265.6 11.4 %collective-permute-start.6 = (bf16[2,1,80,768]{2,3,1,0:T(8,128)(2,1)S(1)}, bf16[2,1,80,768]{2,3,1,0:T(8,128)(2,1)S(1)}, u32[]{:S(2)}, u32[]{:S(2)}) collective-permute-start(bf16[2,1,80,768]{2,3,1,0:T(8,128)(2,1)S(1)} %fusion.42), channel_id=1, source_target_pairs={{0,4},{4,0},{1,5},{5,1},{2,6},{6,2},{3,7},{7,3},{8,12},{12,8},{9,1... | collective-permute-start | bytes 737288 | tf_op jit(solution)/shard_map/ppermute | solution.py:24
  277.2 12.2 %collective-permute-start.7 = (bf16[2,1,80,768]{2,3,1,0:T(8,128)(2,1)S(1)}, bf16[2,1,80,768]{2,3,1,0:T(8,128)(2,1)S(1)}, u32[]{:S(2)}, u32[]{:S(2)}) collective-permute-start(bf16[2,1,80,768]{2,3,1,0:T(8,128)(2,1)S(1)} %fusion.11), channel_id=1, source_target_pairs={{0,8},{8,0},{1,9},{9,1},{2,10},{10,2},{3,11},{11,3},{4,12},{12,4},... | collective-permute-start | bytes 737288 | tf_op jit(solution)/shard_map/ppermute | solution.py:24
Sparse Core Ops, SparseCore 0:
  78.4 41.0 all-gather.4
  121.6 23.7 all-gather.6
  163.9 213.1 reduce-scatter.3
where the time goes:
time: 387 us; the launch traced here: 386 us
  waiting for transfers between devices  235 us (61%)
  starting transfers between devices  80.7 us (21%)
  local copies, waits for them, and re-layouts  17.3 us (4%)
  between operations  17.3 us (4%)
  blocking collectives  16.4 us (4%)
  matrix products  12 us (3%)
  other arithmetic  8.17 us (2%)
    ppermute x8, waiting for transfers between devices, swapped(): return lax.ppermute(block, axis, route)  100 us
    unnamed x4, waiting for transfers between devices  86.2 us
    ppermute x8, starting transfers between devices, swapped(): return lax.ppermute(block, axis, route)  50 us
    all_gather x2, waiting for transfers between devices, stacked_from(): tiles = lax.all_gather(tiles, axes[k])  47.8 us
    all_gather x1, blocking collectives, stacked_from(): tiles = lax.all_gather(tiles, axes[k])  16.4 us
    all_to_all x1, starting transfers between devices, sent_together(): lax.all_to_all(both, axis, split_axis=split_dim, concat_axis=concat_dim,...  15.4 us
    all_to_all x1, starting transfers between devices, local(): lax.all_to_all(part_rows, 'expert', split_axis=0, concat_axis=0, tiled=True)  15.2 us
    unnamed x18, local copies, waits for them, and re-layouts  10.3 us
  transfers between devices with their start and end apart: 13, of which 11 were waited for; matrix products, arithmetic and copies ran while one was open for 5% of the time, Pallas kernels for 0%

commit v1 on v0

v1 whole, which is shorter than its diff:
```python
import jax
import jax.numpy as jnp
from jax import lax
from jax.sharding import Mesh
from jax.sharding import PartitionSpec as P

HSPLIT = 4
CAP = 8
AXES = ("y", "zl", "core", "x", "zh")
DP = ("y", "zl", "core")
EXPERT = ("x", "zh")
RING = ("zh", "zl")
PLANE = ("x", "y")
SPREAD = ("y", "core")

first_decay = 0.9
second_decay = 0.999


def partner_copy(block, mask, count):
    def branch(k):
        return lambda v: lax.ppermute(v, EXPERT, [(i, i ^ k) for i in range(count)])

    return lax.switch(mask - 1, [branch(k) for k in range(1, count)], block)


def local(tokens, cotangent, routes, gates, layout, weights, first_moment, second_moment):
    n_x, n_zh = lax.axis_size("x"), lax.axis_size("zh")
    n_y, n_zl, n_core = lax.axis_size("y"), lax.axis_size("zl"), lax.axis_size("core")
    n_expert = n_x * n_zh
    own_index = lax.axis_index(EXPERT)
    core = lax.axis_index("core")
    lane_ids = jnp.arange(n_expert, dtype=jnp.int32)
    placement = layout[0]
    mask = layout[1, 0]
    swap_on = layout[2]
    inverse = jnp.sum(
        jnp.where(placement[None, :] == lane_ids[:, None], lane_ids[None, :], 0), axis=1
    )
    slot_owner = inverse // HSPLIT
    active = jnp.sum(jnp.where(lane_ids == own_index, swap_on, 0)) == 1

    depth, wide = weights.shape[1:]
    half = wide // 3 // n_core
    w = weights[0].reshape(depth, 3, n_core, half).transpose(2, 0, 1, 3)
    w = w.reshape(n_core, depth, 3 * half)
    w = lax.all_gather(w, RING).reshape(n_zh, n_zl, n_core, depth, 3 * half)
    w = w.transpose(0, 2, 1, 3, 4).reshape(n_zh * n_core, n_zl, depth, 3 * half)
    w = lax.all_to_all(w, SPREAD, split_axis=0, concat_axis=0, tiled=True)
    w = w.reshape(n_y, n_core, n_zl, depth, 3 * half).transpose(0, 2, 1, 3, 4)
    w = w.reshape(-1, 3 * half)

    moments = jnp.stack((first_moment[0], second_moment[0]))
    moved = partner_copy(moments.astype(jnp.bfloat16), mask, n_expert)
    held = jnp.where(active, moved.astype(jnp.float32), moments)

    n_window = n_expert // HSPLIT
    tok_dev, top_count = routes.shape
    width = tokens.shape[1]
    flat_ids = routes.reshape(-1)
    window_ids = jnp.arange(n_window, dtype=jnp.int32)
    hit_table = (flat_ids[:, None] == window_ids[None, :]).astype(jnp.int32)
    earlier = jnp.cumsum(hit_table, axis=0) - hit_table
    position = jnp.sum(earlier * hit_table, axis=1)
    kept = (flat_ids < n_window) & (position < CAP)
    slot_key = jnp.where(kept, flat_ids * CAP + position, -1)
    slot_pick = (jnp.arange(n_window * CAP, dtype=jnp.int32)[:, None] == slot_key[None, :]).astype(
        jnp.float32
    )
    assign_rows = jnp.arange(tok_dev * top_count, dtype=jnp.int32)[:, None] // top_count
    assign_token = (assign_rows == jnp.arange(tok_dev, dtype=jnp.int32)[None, :]).astype(
        jnp.float32
    )
    slot_token = jnp.dot(slot_pick, assign_token, precision=lax.Precision.HIGHEST)
    slot_gate = jnp.dot(slot_pick, gates.reshape(-1), precision=lax.Precision.HIGHEST)
    choose = (slot_owner[:, None] == window_ids[None, :]).astype(jnp.float32)
    dest_token = jnp.dot(
        choose, slot_token.reshape(n_window, CAP * tok_dev), precision=lax.Precision.HIGHEST
    )
    dest_token = dest_token.reshape(n_expert * CAP, tok_dev).astype(jnp.bfloat16)
    dest_gate = jnp.dot(
        choose, slot_gate.reshape(n_window, CAP), precision=lax.Precision.HIGHEST
    ).reshape(-1, 1)
    send_rows = jnp.dot(dest_token, tokens, preferred_element_type=jnp.float32).astype(jnp.bfloat16)
    send_grads = (
        jnp.dot(dest_token, cotangent, preferred_element_type=jnp.float32) * dest_gate
    ).astype(jnp.bfloat16)
    send = jnp.concatenate(
        (send_rows.reshape(n_expert, CAP, width), send_grads.reshape(n_expert, CAP, width)), axis=1
    )
    got = lax.all_to_all(send, PLANE, split_axis=0, concat_axis=0, tiled=True)
    got = lax.all_gather(got, "core")
    rows_in = got[:, :, :CAP].reshape(-1, width)
    grads_in = got[:, :, CAP:].reshape(-1, width)

    pre_act = jnp.dot(rows_in, w[:, : 2 * half], preferred_element_type=jnp.float32)
    hidden_grad = jnp.dot(grads_in, w[:, 2 * half :], preferred_element_type=jnp.float32)
    gate_pre = pre_act[:, :half]
    up_pre = pre_act[:, half:]
    sigma = jax.nn.sigmoid(gate_pre)
    active_part = gate_pre * sigma
    hidden = (active_part * up_pre).astype(jnp.bfloat16)
    gate_grad = (hidden_grad * up_pre * sigma * (1.0 + gate_pre * (1.0 - sigma))).astype(
        jnp.bfloat16
    )
    up_grad = (hidden_grad * active_part).astype(jnp.bfloat16)
    both_grads = jnp.concatenate((gate_grad, up_grad), axis=1)

    proj_grad = lax.dot_general(
        rows_in, both_grads, (((0,), (0,)), ((), ())), preferred_element_type=jnp.float32
    )
    down_grad = lax.dot_general(
        grads_in, hidden, (((0,), (0,)), ((), ())), preferred_element_type=jnp.float32
    )
    g = jnp.concatenate((proj_grad, down_grad), axis=1).astype(jnp.bfloat16)
    g = g.reshape(n_y, n_zl, n_core, depth, 3 * half).transpose(0, 2, 1, 3, 4)
    g = g.reshape(n_y * n_core, n_zl, depth, 3 * half)
    g = lax.all_to_all(g, SPREAD, split_axis=0, concat_axis=0, tiled=True)
    g = g.reshape(n_zh, n_core, n_zl, depth, 3 * half).transpose(0, 2, 1, 3, 4)
    g = g.reshape(n_zh * n_zl * n_core * depth, 3 * half)

    part = lax.dot_general(
        both_grads,
        w[:, : 2 * half],
        (((1,), (1,)), ((), ())),
        preferred_element_type=jnp.float32,
    )
    part = part.astype(jnp.bfloat16).reshape(n_core, n_expert * CAP, width)
    theirs = jnp.where(core == 0, part[1], part[0])
    mine = jnp.where(core == 0, part[0], part[1])
    theirs = lax.ppermute(theirs, "core", [(0, 1), (1, 0)])
    part = (mine.astype(jnp.float32) + theirs.astype(jnp.float32)).astype(jnp.bfloat16)
    part = part.reshape(n_expert, CAP, width)
    returned = lax.all_to_all(part, PLANE, split_axis=0, concat_axis=0, tiled=True)
    grad_input = lax.dot_general(
        dest_token,
        returned.reshape(-1, width),
        (((0,), (0,)), ((), ())),
        preferred_element_type=jnp.float32,
    ).astype(jnp.bfloat16)

    g = lax.psum_scatter(g, RING, scatter_dimension=0, tiled=True)
    g = g.reshape(n_core, depth, 3, half).transpose(1, 2, 0, 3).reshape(depth, wide)
    g_moved = partner_copy(g, mask, n_expert)
    g = jnp.where(active, g_moved, g).astype(jnp.float32)
    new_first = first_decay * held[0] + (1.0 - first_decay) * g
    new_second = second_decay * held[1] + (1.0 - second_decay) * g * g
    return (grad_input, new_first[None], new_second[None])


def solution(mesh):
    split = Mesh(mesh.devices.reshape(4, 4, 2, 4, 4), AXES)
    rows = P(DP + EXPERT, None)
    slots = P(EXPERT, DP, None)
    return jax.shard_map(
        local,
        mesh=split,
        in_specs=(rows, rows, rows, rows, P(), slots, slots, slots),
        out_specs=(rows, slots, slots),
        check_vma=False,
    )
```

time: 387 us -> 270 us (0.70)
  the two profiles are of different devices: /device:TPU:4 before, /device:TPU:144 now
where the time goes in v1:
time: 270 us
  waiting for transfers between devices  133 us (49%)
  blocking collectives  52.9 us (20%)
  starting transfers between devices  33.5 us (12%)
  local copies, waits for them, and re-layouts  23.1 us (9%)
  between operations  15.4 us (6%)
  other arithmetic  6.46 us (2%)
  matrix products  5.85 us (2%)
    all_gather x1, waiting for transfers between devices, local(): w = lax.all_gather(w, RING).reshape(n_zh, n_zl, n_core, depth, 3 * half)  43.8 us
    ppermute x2, waiting for transfers between devices, branch(): return lambda v: lax.ppermute(v, EXPERT, [(i, i ^ k) for i in range(count)])  39.4 us
    reduce_scatter x1, waiting for transfers between devices, local(): g = lax.psum_scatter(g, RING, scatter_dimension=0, tiled=True)  32.1 us
    all_to_all x1, blocking collectives, local(): g = lax.all_to_all(g, SPREAD, split_axis=0, concat_axis=0, tiled=True)  27.9 us
    all_to_all x1, blocking collectives, local(): got = lax.all_to_all(send, PLANE, split_axis=0, concat_axis=0, tiled=True)  25 us
    ppermute x2, starting transfers between devices, branch(): return lambda v: lax.ppermute(v, EXPERT, [(i, i ^ k) for i in range(count)])  19.2 us
    all_gather x1, waiting for transfers between devices, local(): got = lax.all_gather(got, 'core')  15.3 us
    all_to_all x1, starting transfers between devices, local(): lax.all_to_all(part, PLANE, split_axis=0, concat_axis=0, tiled=True)  7.52 us
  transfers between devices with their start and end apart: 8, of which 6 were waited for; matrix products, arithmetic and copies ran while one was open for 8% of the time, Pallas kernels for 0%

profile of v1, /device:TPU:144, one launch (start us, length us, event | category | flops | bytes accessed | tf_op | source)
XLA Modules:
  0.0 270.1 jit_solution(11932634944346325634)
XLA Ops:
  7.2 1.0 reshape_squeeze.3
  8.3 0.8 all_gather_reshape.3
  9.1 0.8 copy.70
  10.2 1.1 reduce-window.6
  11.4 0.2 slice_reduce_fusion
  11.9 0.3 fusion.10
  12.3 0.2 convolution_convert_fusion.5
  12.9 0.5 fusion.20
  13.7 0.3 fusion.2
  14.0 0.3 fusion.1
  14.5 25.0 %all_to_all.20 = bf16[16,16,2560]{2,1,0:T(8,128)(2,1)} all-to-all(bf16[16,16,2560]{2,1,0:T(8,128)(2,1)S(1)} %pad_maximum_fusion), channel_id=1, replica_groups=mesh['y'=4,'zl'=4,'core'=2,'x'=4,'zh'=4] {'x','y'}, dimensions={0} | all-to-all | bytes 2621440 | tf_op jit(solution)/shard_map/all_to_all | solution.py:91
  39.5 43.8 %all-gather.4.cloned.1.call-done = bf16[16,2,80,384]{3,2,1,0:T(8,128)(2,1)} async-done(((bf16[1,2,80,384]{3,2,1,0:T(8,128)(2,1)}), bf16[16,2,80,384]{3,2,1,0:T(8,128)(2,1)}) %all-gather.4.cloned.1.call-update) | async-done | bytes 1966096 | tf_op jit(solution)/shard_map/all_gather | solution.py:47
  83.4 3.1 %copy.75 = bf16[4,2,4,80,384]{4,3,2,1,0:T(8,128)(2,1)} copy(bf16[4,2,4,80,384]{4,3,1,2,0:T(8,128)(2,1)} %bitcast.108) | data formatting | bytes 3932160 | tf_op jit(solution)/shard_map/transpose | solution.py:48
  86.4 4.8 %all-to-all-start.1 = ((bf16[8,4,80,384]{3,2,1,0:T(8,128)(2,1)}), bf16[8,4,80,384]{3,2,1,0:T(8,128)(2,1)S(1)}, u32[]{:S(2)}, u32[]{:S(2)}) async-start(bf16[8,4,80,384]{3,2,1,0:T(8,128)(2,1)} %bitcast.95), calls=%async_computation.1 | async-start | bytes 3932160 | tf_op jit(solution)/shard_map/all_to_all | solution.py:49
  91.2 15.3 %all-gather.6.cloned.1.call-done = bf16[32,16,2560]{2,1,0:T(8,128)(2,1)} async-done(((bf16[16,16,2560]{2,1,0:T(8,128)(2,1)}), bf16[32,16,2560]{2,1,0:T(8,128)(2,1)}) %all-gather.6.cloned.1.call-update) | async-done | bytes 2621456 | tf_op jit(solution)/shard_map/all_gather | solution.py:92
  106.5 3.4 %fusion.42 = (bf16[2,16,8,2560]{3,2,1,0:T(8,128)(2,1)}, bf16[2,16,8,2560]{3,2,1,0:T(8,128)(2,1)}) fusion(bf16[2,16,16,2560]{3,2,1,0:T(8,128)(2,1)} %bitcast.107), kind=kLoop, calls=%fused_computation.87 | loop fusion | bytes 5242880 | tf_op jit(solution)/shard_map/slice | solution.py:93
  109.9 2.5 copy.77
  112.4 2.5 copy.79
  114.9 0.2 copy.76
  115.1 1.5 copy-done.4
  116.6 0.6 fusion.4
  117.2 0.7 copy-done.3
  117.9 0.6 multiply_convert_fusion.2
  118.5 0.7 copy-done.6
  119.2 0.5 convolution_convert_fusion.4
  119.9 0.5 convolution_convert_fusion.3
  120.7 0.2 copy.81
  120.9 27.9 %all_to_all.21 = bf16[8,4,80,384]{3,2,1,0:T(8,128)(2,1)S(1)} all-to-all(bf16[8,4,80,384]{3,2,1,0:T(8,128)(2,1)S(1)} %bitcast.96), channel_id=1, replica_groups=mesh['y'=4,'zl'=4,'core'=2,'x'=4,'zh'=4] {'y','core'}, dimensions={0} | all-to-all | bytes 3932160 | tf_op jit(solution)/shard_map/all_to_all | solution.py:118
  148.8 1.5 copy.82
  150.3 1.5 copy-done.2
  151.9 0.6 convolution_convert_fusion
  152.5 1.9 collective-permute-start.30
  154.4 2.1 collective-permute-done.30
  156.5 1.1 fusion.6
  157.6 7.5 %all-to-all-start.2 = ((bf16[16,8,2560]{2,1,0:T(8,128)(2,1)}), bf16[16,8,2560]{2,1,0:T(8,128)(2,1)S(1)}, u32[]{:S(2)}, u32[]{:S(2)}) async-start(bf16[16,8,2560]{2,1,0:T(8,128)(2,1)} %fusion.6), calls=%async_computation.2 | async-start | bytes 1310720 | tf_op jit(solution)/shard_map/all_to_all | solution.py:134
  165.1 0.5 slice.62
  166.4 0.6 fusion.38
  167.6 37.0 %conditional.5 = (bf16[2,80,768]{2,1,0:T(8,128)(2,1)}) conditional(s32[]{:T(128)} %bitcast.20, bf16[2,80,768]{2,1,0:T(8,128)(2,1)S(1)} %convert_element_type.148, bf16[2,80,768]{2,1,0:T(8,128)(2,1)S(1)} %convert_element_type.148, bf16[2,80,768]{2,1,0:T(8,128)(2,1)S(1)} %convert_element_type.148, ...), branch_computations={%region_5.6_spmd, %region_6.7_spmd, %region_7.8_spmd, %region_8.9_... | conditional | bytes 983088
  167.7 10.1 %collective-permute-start.13 = (bf16[2,80,768]{2,1,0:T(8,128)(2,1)S(1)}, bf16[2,80,768]{2,1,0:T(8,128)(2,1)}, u32[]{:S(2)}, u32[]{:S(2)}) collective-permute-start(bf16[2,80,768]{2,1,0:T(8,128)(2,1)S(1)} %param.13), channel_id=1, source_target_pairs={{0,14},{1,15},{2,12},{3,13},{4,10},{5,11},{6,8},{7,9},{8,6},{9,7},... | collective-permute-start | bytes 737288 | tf_op jit(solution)/shard_map/cond/branch_13_fun/ppermute | solution.py:22
  177.8 26.8 %collective-permute-done.13 = bf16[2,80,768]{2,1,0:T(8,128)(2,1)} collective-permute-done((bf16[2,80,768]{2,1,0:T(8,128)(2,1)S(1)}, bf16[2,80,768]{2,1,0:T(8,128)(2,1)}, u32[]{:S(2)}, u32[]{:S(2)}) %collective-permute-start.13) | collective-permute-done | bytes 245792 | tf_op jit(solution)/shard_map/cond/branch_13_fun/ppermute | solution.py:22
  204.6 1.0 convert_select_fusion
  205.6 1.2 convolution_convert_fusion.1
  206.8 32.1 %reduce-scatter.2.cloned.1.call-done = bf16[160,384]{1,0:T(8,128)(2,1)} async-done(((bf16[2560,384]{1,0:T(8,128)(2,1)}), bf16[160,384]{1,0:T(8,128)(2,1)}) %reduce-scatter.2.cloned.1.call-update) | async-done | bytes 122896 | tf_op jit(solution)/shard_map/reduce_scatter | solution.py:142
  238.9 0.9 reshape.237
  240.1 21.7 %conditional.6 = (bf16[80,768]{1,0:T(8,128)(2,1)}) conditional(s32[]{:T(128)} %bitcast.20, bf16[80,768]{1,0:T(8,128)(2,1)S(1)} %reshape.238, bf16[80,768]{1,0:T(8,128)(2,1)S(1)} %reshape.238, bf16[80,768]{1,0:T(8,128)(2,1)S(1)} %reshape.238, bf16[80,768]{1,0:T(8,128)(2,1)S(1)} %reshape.238, ...), branch_computations={%region_21.22_spmd, %region_22.23_spmd, %region_23.24_spmd, %regio... | conditional | bytes 491568 | solution.py:24
  240.1 9.0 %collective-permute-start.28 = (bf16[80,768]{1,0:T(8,128)(2,1)S(1)}, bf16[80,768]{1,0:T(8,128)(2,1)}, u32[]{:S(2)}, u32[]{:S(2)}) collective-permute-start(bf16[80,768]{1,0:T(8,128)(2,1)S(1)} %param.28), channel_id=1, source_target_pairs={{0,14},{1,15},{2,12},{3,13},{4,10},{5,11},{6,8},{7,9},{8,6},{9,7},... | collective-permute-start | bytes 368648 | tf_op jit(solution)/shard_map/cond/branch_13_fun/ppermute | solution.py:22
  249.2 12.6 %collective-permute-done.28 = bf16[80,768]{1,0:T(8,128)(2,1)} collective-permute-done((bf16[80,768]{1,0:T(8,128)(2,1)S(1)}, bf16[80,768]{1,0:T(8,128)(2,1)}, u32[]{:S(2)}, u32[]{:S(2)}) %collective-permute-start.28) | collective-permute-done | bytes 122912 | tf_op jit(solution)/shard_map/cond/branch_13_fun/ppermute | solution.py:22
  261.8 1.8 fusion.14
  (54 shorter events, 2.4 us)
Async XLA Ops:
  7.2 6.5 %copy-start = (bf16[128,2560]{1,0:T(8,128)(2,1)S(1)}, bf16[128,2560]{1,0:T(8,128)(2,1)}, u32[]{:S(2)}) copy-start(bf16[128,2560]{1,0:T(8,128)(2,1)} %param.38) | copy-start | bytes 1966084
  7.2 5.0 %copy-start.11 = (s32[3,16]{1,0:T(4,128)S(1)}, s32[3,16]{1,0:T(4,128)}, u32[]{:S(2)}) copy-start(s32[3,16]{1,0:T(4,128)} %param.42) | copy-start | bytes 580
  7.2 5.4 %copy-start.10 = (f32[128,6]{0,1:T(8,128)S(1)}, f32[128,6]{0,1:T(8,128)}, u32[]{:S(2)}) copy-start(f32[128,6]{0,1:T(8,128)} %param.41) | copy-start | bytes 9220
  7.2 76.2 %all-gather.4.cloned.1.call-start = ((), (), s32[]{:S(2)}) async-start(), calls=%async_computation.5 | async-start | bytes 2088960 | tf_op jit(solution)/shard_map/all_gather | solution.py:47
  8.3 5.7 %copy-start.7 = (bf16[128,2560]{1,0:T(8,128)(2,1)S(1)}, bf16[128,2560]{1,0:T(8,128)(2,1)}, u32[]{:S(2)}) copy-start(bf16[128,2560]{1,0:T(8,128)(2,1)} %param.39) | copy-start | bytes 1966084
  9.1 97.4 %all-gather.6.cloned.1.call-start = ((), (), s32[]{:S(2)}) async-start(), calls=%async_computation.7 | async-start | bytes 3932160 | tf_op jit(solution)/shard_map/all_gather | solution.py:92
  86.4 28.4 %all-to-all-start.1 = ((bf16[8,4,80,384]{3,2,1,0:T(8,128)(2,1)}), bf16[8,4,80,384]{3,2,1,0:T(8,128)(2,1)S(1)}, u32[]{:S(2)}, u32[]{:S(2)}) async-start(bf16[8,4,80,384]{3,2,1,0:T(8,128)(2,1)} %bitcast.95), calls=%async_computation.1 | async-start | bytes 3932160 | tf_op jit(solution)/shard_map/all_to_all | solution.py:49
  91.2 147.7 %reduce-scatter.2.cloned.1.call-start = ((), (), s32[]{:S(2)}) async-start(), calls=%async_computation.6 | async-start | bytes 2088960 | tf_op jit(solution)/shard_map/reduce_scatter | solution.py:142
  114.9 1.7 copy-start.4
  115.1 2.1 copy-start.1
  116.6 1.3 copy-start.3
  117.9 1.3 copy-start.6
  118.5 1.4 copy-start.5
  150.3 1.5 copy-start.2
  152.5 4.0 %collective-permute-start.30 = (bf16[128,2560]{1,0:T(8,128)(2,1)S(1)}, bf16[128,2560]{1,0:T(8,128)(2,1)S(1)}, u32[]{:S(2)}, u32[]{:S(2)}) collective-permute-start(bf16[128,2560]{1,0:T(8,128)(2,1)S(1)} %broadcast_select_fusion), channel_id=1, source_target_pairs={{0,16},{16,0},{1,17},{17,1},{2,18},{18,2},{3,19},{19,3},{4,20},{20... | collective-permute-start | bytes 1966088 | tf_op jit(solution)/shard_map/ppermute | solution.py:131
  157.6 8.0 %copy-start.8 = (f32[1,80,768]{2,1,0:T(8,128)S(1)}, f32[1,80,768]{2,1,0:T(8,128)}, u32[]{:S(2)}) copy-start(f32[1,80,768]{2,1,0:T(8,128)} %param.44) | copy-start | bytes 737284
  157.6 8.1 %copy-start.9 = (f32[1,80,768]{2,1,0:T(8,128)S(1)}, f32[1,80,768]{2,1,0:T(8,128)}, u32[]{:S(2)}) copy-start(f32[1,80,768]{2,1,0:T(8,128)} %param.45) | copy-start | bytes 737284
  157.6 48.0 %all-to-all-start.2 = ((bf16[16,8,2560]{2,1,0:T(8,128)(2,1)}), bf16[16,8,2560]{2,1,0:T(8,128)(2,1)S(1)}, u32[]{:S(2)}, u32[]{:S(2)}) async-start(bf16[16,8,2560]{2,1,0:T(8,128)(2,1)} %fusion.6), calls=%async_computation.2 | async-start | bytes 1310720 | tf_op jit(solution)/shard_map/all_to_all | solution.py:134
  167.7 36.9 %collective-permute-start.13 = (bf16[2,80,768]{2,1,0:T(8,128)(2,1)S(1)}, bf16[2,80,768]{2,1,0:T(8,128)(2,1)}, u32[]{:S(2)}, u32[]{:S(2)}) collective-permute-start(bf16[2,80,768]{2,1,0:T(8,128)(2,1)S(1)} %param.13), channel_id=1, source_target_pairs={{0,14},{1,15},{2,12},{3,13},{4,10},{5,11},{6,8},{7,9},{8,6},{9,7},... | collective-permute-start | bytes 737288 | tf_op jit(solution)/shard_map/cond/branch_13_fun/ppermute | solution.py:22
  240.1 21.7 %collective-permute-start.28 = (bf16[80,768]{1,0:T(8,128)(2,1)S(1)}, bf16[80,768]{1,0:T(8,128)(2,1)}, u32[]{:S(2)}, u32[]{:S(2)}) collective-permute-start(bf16[80,768]{1,0:T(8,128)(2,1)S(1)} %param.28), channel_id=1, source_target_pairs={{0,14},{1,15},{2,12},{3,13},{4,10},{5,11},{6,8},{7,9},{8,6},{9,7},... | collective-permute-start | bytes 368648 | tf_op jit(solution)/shard_map/cond/branch_13_fun/ppermute | solution.py:22
Sparse Core Ops, SparseCore 0:
  10.7 72.6 all-gather.3
  85.4 21.0 all-gather.5
  150.5 88.3 reduce-scatter.1
